TPU v7x, 512 devices: a whole 4x4x16 slice. The times are simulated.
512 devices in a mesh: dp: 16 (over z), expert: 32 (over x, y, core).
Axes of the slice: x: 4, y: 4, z: 16, core: 2. Of those that a mesh axis runs over, the one named last changes fastest.
Arguments:
- tokens: bfloat16 [4096, 4096], P('expert', 'dp'), may hold values from -6 to 6
- route_ids: int32 [4096, 8], P('expert'), may hold values from 0 to 31, all different within a row; in each aligned block of 128 rows (0 to 127, 128 to 255, ...) at most 40 rows name the same one
- route_weights: bfloat16 [4096, 8], P('expert'), may hold values from 0.099609375 to 0.3984375
- gate_weight: bfloat16 [32, 4096, 768], P('expert', 'dp'), may hold values from -0.09375 to 0.09375
- up_weight: bfloat16 [32, 4096, 768], P('expert', 'dp'), may hold values from -0.09375 to 0.09375
- down_weight: bfloat16 [32, 768, 4096], P('expert', None, 'dp'), may hold values from -0.21875 to 0.21875
- out_grad: bfloat16 [4096, 4096], P('expert', 'dp'), may hold values from -3 to 3
Outputs:
- mixed: bfloat16 [4096, 4096], P('expert', 'dp')
- input_grad: bfloat16 [4096, 4096], P('expert', 'dp')
- gate_weight_grad: float32 [32, 4096, 768], P('expert', 'dp')
- up_weight_grad: float32 [32, 4096, 768], P('expert', 'dp')
- down_weight_grad: float32 [32, 768, 4096], P('expert', None, 'dp')
Inputs may be any that keep to these rules, and one draw needn't show every extreme that they name: `route_ids`: each row names 8 different experts. In each aligned block of 128 rows (the tokens of one index of expert) no expert is named by more than 40 rows, a bound that some block reaches.
All inputs are finite; a program needn't handle non-finite values.
Results may differ from a plain program's by a relative error of at most 0.039.
Values may be sent and summed in bfloat16 or wider, within the bound.
A program may use at most 64 MiB of HBM per device.

v0:
```python
import jax
import jax.numpy as jnp
from jax import lax
from jax.sharding import PartitionSpec as P


def contract_rows(first_op, second_op):
    return lax.dot_general(
        first_op, second_op, (((0,), (0,)), ((), ())), preferred_element_type=jnp.float32
    )


def contract_cols(first_op, second_op):
    return lax.dot_general(
        first_op, second_op, (((1,), (1,)), ((), ())), preferred_element_type=jnp.float32
    )


def expert_forward(expert_rows, weight_g, weight_u, weight_d):
    partial_gate = jnp.dot(expert_rows, weight_g, preferred_element_type=jnp.float32)
    partial_up = jnp.dot(expert_rows, weight_u, preferred_element_type=jnp.float32)
    gate_pre, up_pre = (
        lax.psum(partial_gate.astype(jnp.bfloat16), "dp").astype(jnp.float32),
        lax.psum(partial_up.astype(jnp.bfloat16), "dp").astype(jnp.float32),
    )
    hidden = (jax.nn.silu(gate_pre) * up_pre).astype(jnp.bfloat16)
    produced = jnp.dot(hidden, weight_d, preferred_element_type=jnp.float32).astype(jnp.bfloat16)
    return (gate_pre, up_pre, hidden, produced)


def expert_backward(expert_rows, upstream, gate_pre, up_pre, hidden, weight_g, weight_u, weight_d):
    partial_value = contract_cols(upstream, weight_d)
    hidden_grad = lax.psum(partial_value.astype(jnp.bfloat16), "dp").astype(jnp.float32)
    sigmoid_gate = jax.nn.sigmoid(gate_pre)
    gate_delta = (
        hidden_grad * up_pre * sigmoid_gate * (1.0 + gate_pre * (1.0 - sigmoid_gate))
    ).astype(jnp.bfloat16)
    up_delta = (hidden_grad * jax.nn.silu(gate_pre)).astype(jnp.bfloat16)
    down_grad = contract_rows(hidden, upstream)
    gate_grad = contract_rows(expert_rows, gate_delta)
    up_grad = contract_rows(expert_rows, up_delta)
    back_rows = (contract_cols(gate_delta, weight_g) + contract_cols(up_delta, weight_u)).astype(
        jnp.bfloat16
    )
    return (gate_grad, up_grad, down_grad, back_rows)


def shards(tokens, route_ids, route_weights, gate_weight, up_weight, down_weight, out_grad):
    expert_count = lax.axis_size("expert")
    tok_count = tokens.shape[0]
    width = tokens.shape[1]
    top_count = route_ids.shape[1]
    capacity = min(tok_count, tok_count * top_count // expert_count + tok_count // 16)
    row_total = expert_count * capacity
    weight_g = gate_weight[0]
    weight_u = up_weight[0]
    weight_d = down_weight[0]
    every_tok, every_grad, every_weight = (
        lax.all_gather(tokens, "expert", axis=0, tiled=True),
        lax.all_gather(out_grad, "expert", axis=0, tiled=True),
        lax.all_gather(route_weights, "expert", axis=0, tiled=True),
    )
    every_ids = lax.all_gather(route_ids, "expert", axis=0, tiled=True)
    my_expert = lax.axis_index("expert")
    chosen = every_ids == my_expert
    hit_count = jnp.sum(chosen.astype(jnp.int32), axis=1).reshape(expert_count, tok_count)
    hit_rank = jnp.cumsum(hit_count, axis=1) - hit_count
    block_start = (jnp.arange(expert_count, dtype=jnp.int32) * capacity)[:, None]
    dest_row = jnp.where(hit_count > 0, block_start + hit_rank, row_total).reshape(-1)
    tok_weight = jnp.sum(jnp.where(chosen, every_weight.astype(jnp.float32), 0.0), axis=1)
    expert_rows = (
        jnp.zeros((row_total, width), jnp.bfloat16).at[dest_row].set(every_tok, mode="drop")
    )
    row_weight = jnp.zeros((row_total,), jnp.float32).at[dest_row].set(tok_weight, mode="drop")
    gate_pre, up_pre, hidden, produced = expert_forward(expert_rows, weight_g, weight_u, weight_d)
    safe_row = jnp.minimum(dest_row, row_total - 1)
    present = (hit_count.reshape(-1) > 0).astype(jnp.float32)[:, None]
    weighted = (
        (row_weight[:, None] * produced.astype(jnp.float32))
        .astype(jnp.bfloat16)
        .astype(jnp.float32)
    )
    mixed = lax.psum_scatter(
        (weighted[safe_row] * present).astype(jnp.bfloat16),
        "expert",
        scatter_dimension=0,
        tiled=True,
    )
    grad_rows = (
        jnp.zeros((row_total, width), jnp.bfloat16).at[dest_row].set(every_grad, mode="drop")
    )
    upstream = (row_weight[:, None] * grad_rows.astype(jnp.float32)).astype(jnp.bfloat16)
    gate_grad, up_grad, down_grad, back_rows = expert_backward(
        expert_rows, upstream, gate_pre, up_pre, hidden, weight_g, weight_u, weight_d
    )
    input_grad = lax.psum_scatter(
        (back_rows.astype(jnp.float32)[safe_row] * present).astype(jnp.bfloat16),
        "expert",
        scatter_dimension=0,
        tiled=True,
    )
    return (mixed, input_grad, gate_grad[None], up_grad[None], down_grad[None])


def solution(mesh):
    return jax.shard_map(
        shards,
        mesh=mesh,
        in_specs=(
            P("expert", "dp"),
            P("expert", None),
            P("expert", None),
            P("expert", "dp", None),
            P("expert", "dp", None),
            P("expert", None, "dp"),
            P("expert", "dp"),
        ),
        out_specs=(
            P("expert", "dp"),
            P("expert", "dp"),
            P("expert", "dp", None),
            P("expert", "dp", None),
            P("expert", None, "dp"),
        ),
        check_vma=False,
    )
```

profile of v0, /device:TPU:1, one launch (start us, length us, event | category | flops | bytes accessed | tf_op | source)
XLA Modules:
  0.0 579.9 jit_solution(8875477676704722195)
XLA Ops:
  7.2 0.7 all-gather.3.cloned.1.call-update
  8.0 0.7 all-gather.5.cloned.1.call-update
  8.7 28.6 %all_gather.13 = bf16[4096,8]{0,1:T(8,128)(2,1)S(1)} all-gather(bf16[128,8]{0,1:T(8,128)(2,1)} %param.9), channel_id=1, replica_groups=mesh['dp'=16,'expert'=32] {'expert'}, dimensions={0}, use_global_device_ids=true | all-gather | bytes 67584 | tf_op jit(solution)/shard_map/all_gather | solution.py:61
  37.3 24.2 %all_gather.12 = s32[4096,8]{0,1:T(8,128)S(1)} all-gather(s32[128,8]{0,1:T(8,128)} %param.8), channel_id=1, replica_groups=mesh['dp'=16,'expert'=32] {'expert'}, dimensions={0}, use_global_device_ids=true | all-gather | bytes 135168 | tf_op jit(solution)/shard_map/all_gather | solution.py:63
  61.6 0.3 reduce_window_sum.13
  62.0 15.5 %scatter_custom_fusion = f32[1280]{0:T(1024)S(1)} fusion(s32[4096]{0:T(1024)S(1)} %bitcast.45, f32[4096]{0:T(1024)S(1)} %get-tuple-element.10, f32[]{:T(128)} %constant.8.clone.1), kind=kCustom, calls=%fused_computation.56 | custom fusion | bytes 5124 | tf_op jit(solution)/shard_map/scatter | solution.py:74
  77.6 18.3 %scatter_custom_fusion.1 = bf16[1280,256]{1,0:T(8,128)(2,1)S(1)} fusion(s32[4096]{0:T(1024)S(1)} %bitcast.46, bf16[4096,256]{1,0:T(8,128)(2,1)} %all-gather.3.cloned.1.call-done, bf16[]{:T(256)} %constant.13.clone.1), kind=kCustom, calls=%fused_computation.46 | custom fusion | bytes 655872 | tf_op jit(solution)/shard_map/scatter | solution.py:72
  95.9 3.2 convolution_convert_fusion.1
  99.1 2.0 convolution_convert_fusion.2
  101.0 36.2 %all-gather.5.cloned.1.call-done = bf16[4096,256]{1,0:T(8,128)(2,1)} async-done(((bf16[128,256]{1,0:T(8,128)(2,1)}), bf16[4096,256]{1,0:T(8,128)(2,1)}) %all-gather.5.cloned.1.call-update) | async-done | bytes 2097168 | tf_op jit(solution)/shard_map/all_gather | solution.py:60
  137.3 18.3 %scatter_custom_fusion.2 = bf16[1280,256]{1,0:T(8,128)(2,1)S(1)} fusion(s32[4096]{0:T(1024)S(1)} %bitcast.47, bf16[4096,256]{1,0:T(8,128)(2,1)} %all-gather.5.cloned.1.call-done, bf16[]{:T(256)} %constant.13.clone.1), kind=kCustom, calls=%fused_computation.44 | custom fusion | bytes 655872 | tf_op jit(solution)/shard_map/scatter | solution.py:90
  155.6 2.0 convolution_convert_fusion
  157.6 0.2 reduce-scatter.5.cloned.1.call-start
  157.9 163.1 %all-reduce.3.cloned.1.call-done = (bf16[1280,768]{1,0:T(8,128)(2,1)}, bf16[1280,768]{1,0:T(8,128)(2,1)}, bf16[1280,768]{1,0:T(8,128)(2,1)}) async-done(((bf16[1280,768]{1,0:T(8,128)(2,1)}, bf16[1280,768]{1,0:T(8,128)(2,1)}, bf16[1280,768]{1,0:T(8,128)(2,1)}), (bf16[1280,768]{1,0:T(8,128)(2,1)}, bf16[1280,768]{1,0:T(8,128)(2,1)}, bf16[1280,768]{1,0:T(8,128)(2,1)})) %all-reduce.3.cloned.1.call-update) | async-done | bytes 5898256 | tf_op jit(solution)/shard_map/psum | solution.py:24
  321.0 4.2 fusion.4
  325.3 0.7 fusion.12
  326.0 0.7 fusion.19
  326.7 0.4 copy-done.7
  327.1 0.6 copy-done.3
  327.7 0.7 fusion.14
  328.5 16.1 %gather_fusion.1 = f32[4096,256]{1,0:T(8,128)} fusion(f32[1280,256]{1,0:T(8,128)S(1)} %fusion.14, s32[4096]{0:T(1024)S(1)} %broadcast_clamp_fusion), kind=kCustom, calls=%fused_computation.1 | custom fusion | bytes 8404992 | tf_op jit(solution)/shard_map/gather | solution.py:97
  344.6 16.2 %gather_fusion = f32[4096,256]{1,0:T(8,128)} fusion(f32[1280,256]{1,0:T(8,128)S(1)} %fusion.12, s32[4096]{0:T(1024)S(1)} %broadcast_clamp_fusion), kind=kCustom, calls=%fused_computation | custom fusion | bytes 8404992 | tf_op jit(solution)/shard_map/gather | solution.py:84
  360.8 5.1 multiply_convert_fusion
  366.0 0.5 reduce-scatter.3.cloned.1.call-update
  366.5 0.9 copy-done.4
  367.5 0.1 copy-done.6
  367.6 1.6 convolution_bitcast_fusion.1
  369.2 1.6 convolution_bitcast_fusion.2
  370.8 0.2 copy-done.10
  371.0 1.8 convolution_bitcast_fusion
  372.8 94.1 %reduce-scatter.5.cloned.1.call-done = bf16[128,256]{1,0:T(8,128)(2,1)} async-done(((bf16[4096,256]{1,0:T(8,128)(2,1)}), bf16[128,256]{1,0:T(8,128)(2,1)}) %reduce-scatter.5.cloned.1.call-update) | async-done | bytes 65552 | tf_op jit(solution)/shard_map/reduce_scatter | solution.py:96
  466.9 106.4 %reduce-scatter.3.cloned.1.call-done = bf16[128,256]{1,0:T(8,128)(2,1)} async-done(((bf16[4096,256]{1,0:T(8,128)(2,1)}), bf16[128,256]{1,0:T(8,128)(2,1)}) %reduce-scatter.3.cloned.1.call-update) | async-done | bytes 65552 | tf_op jit(solution)/shard_map/reduce_scatter | solution.py:83
  (36 shorter events, 0.5 us)
Async XLA Ops:
  7.2 148.4 %copy-start = (bf16[1,768,256]{2,1,0:T(8,128)(2,1)S(1)}, bf16[1,768,256]{2,1,0:T(8,128)(2,1)}, u32[]{:S(2)}) copy-start(bf16[1,768,256]{2,1,0:T(8,128)(2,1)} %param.12) | copy-start | bytes 1179652
  7.2 70.4 %all-gather.3.cloned.1.call-start = ((), (), s32[]{:S(2)}) async-start(), calls=%async_computation.2 | async-start | bytes 2162688 | tf_op jit(solution)/shard_map/all_gather | solution.py:59
  7.9 129.4 %all-gather.5.cloned.1.call-start = ((), (), s32[]{:S(2)}) async-start(), calls=%async_computation.4 | async-start | bytes 2162688 | tf_op jit(solution)/shard_map/all_gather | solution.py:60
  8.7 312.3 %all-reduce.3.cloned.1.call-start = ((), (), s32[]{:S(2)}) async-start(), calls=%async_computation.6 | async-start | bytes 11796480 | tf_op jit(solution)/shard_map/psum | solution.py:24
  61.5 37.6 %copy-start.11 = (bf16[1,256,768]{2,1,0:T(8,128)(2,1)S(1)}, bf16[1,256,768]{2,1,0:T(8,128)(2,1)}, u32[]{:S(2)}) copy-start(bf16[1,256,768]{2,1,0:T(8,128)(2,1)} %param.10) | copy-start | bytes 1179652
  95.9 5.2 copy-start.5
  155.6 2.0 copy-start.9
  157.6 309.3 %reduce-scatter.5.cloned.1.call-start = ((), (), s32[]{:S(2)}) async-start(), calls=%async_computation.5 | async-start | bytes 2162688 | tf_op jit(solution)/shard_map/reduce_scatter | solution.py:96
  325.2 1.5 copy-start.1
  325.2 1.9 copy-start.7
  325.2 2.5 copy-start.3
  326.0 1.7 copy-start.12
  365.9 1.5 copy-start.4
  365.9 1.7 copy-start.6
  366.0 207.4 %reduce-scatter.3.cloned.1.call-start = ((), (), s32[]{:S(2)}) async-start(), calls=%async_computation.3 | async-start | bytes 2162688 | tf_op jit(solution)/shard_map/reduce_scatter | solution.py:83
  367.6 1.6 copy-start.2
  369.2 1.6 copy-start.8
  369.2 1.8 copy-start.10
Sparse Core Ops, SparseCore 0:
  11.1 64.5 all-gather.2
  78.9 58.3 all-gather.4
  157.8 163.1 all-reduce.2
  366.1 100.7 reduce-scatter.4
  471.7 101.5 reduce-scatter.2
where the time goes:
time: 581 us; the launch traced here: 580 us
  waiting for transfers between devices  402 us (69%)
  local copies, waits for them, and re-layouts  86.8 us (15%)
  blocking collectives  52.7 us (9%)
  matrix products  14.3 us (2%)
  between operations  14 us (2%)
  other arithmetic  9.82 us (2%)
    psum x1, waiting for transfers between devices, expert_forward(): lax.psum(partial_up.astype(jnp.bfloat16), 'dp').astype(jnp.float32)  163 us
    reduce_scatter x1, waiting for transfers between devices, shards(): lax.psum_scatter((weighted[safe_row] * present).astype(jnp.bfloat16), 'ex...  106 us
    reduce_scatter x1, waiting for transfers between devices, shards(): lax.psum_scatter((back_rows.astype(jnp.float32)[safe_row] * present).asty...  94.1 us
    scatter x2, local copies, waits for them, and re-layouts, shards(): jnp.zeros((row_total, width), jnp.bfloat16).at[dest_row]  36.6 us
    all_gather x1, waiting for transfers between devices, shards(): lax.all_gather(out_grad, 'expert', axis=0, tiled=True)  36.2 us
    all_gather x1, blocking collectives, shards(): lax.all_gather(route_weights, 'expert', axis=0, tiled=True)  28.6 us
    all_gather x1, blocking collectives, shards(): every_ids = lax.all_gather(route_ids, 'expert', axis=0, tiled=True)  24.2 us
    gather x1, local copies, waits for them, and re-layouts, shards(): weighted[safe_row] * present  16.2 us
  transfers between devices with their start and end apart: 5, of which 4 were waited for; matrix products, arithmetic and copies ran while one was open for 8% of the time, Pallas kernels for 0%

commit v1 on v0

v1 whole, which is shorter than its diff:
```python
import jax
import jax.numpy as jnp
from jax import lax
from jax.sharding import PartitionSpec as P

SLOT_CHUNKS = (40,)


def dot_of(first_op, second_op, first_dim, second_dim):
    return lax.dot_general(
        first_op,
        second_op,
        (((first_dim,), (second_dim,)), ((), ())),
        preferred_element_type=jnp.float32,
    )


def slot_matrices(route_ids, route_weights, expert_count, capacity):
    tok_count = route_ids.shape[0]
    labels = lax.broadcasted_iota(jnp.int32, (expert_count, 1, 1), 0)
    named = route_ids.T[None, :, :] == labels
    hit = jnp.any(named, axis=1)
    weight = jnp.sum(jnp.where(named, route_weights.astype(jnp.float32).T[None], 0.0), axis=1)
    earlier = lax.broadcasted_iota(jnp.int32, (tok_count, tok_count), 0)
    later = lax.broadcasted_iota(jnp.int32, (tok_count, tok_count), 1)
    before = (earlier < later).astype(jnp.bfloat16)
    rank = dot_of(hit.astype(jnp.bfloat16), before, 1, 0).astype(jnp.int32)
    rank = jnp.where(hit, rank, -1)
    slots = lax.broadcasted_iota(jnp.int32, (expert_count, capacity, tok_count), 1)
    taken = rank[:, None, :] == slots
    place = jnp.where(taken, 1.0, 0.0).astype(jnp.bfloat16)
    scale = jnp.where(taken, weight[:, None, :], 0.0).astype(jnp.bfloat16)
    return place, scale


def swap(rows):
    return lax.all_to_all(rows, "expert", split_axis=0, concat_axis=0, tiled=True)


def pointwise(gate_pre, up_pre, hidden_grad):
    sigmoid_gate = jax.nn.sigmoid(gate_pre)
    silu_gate = gate_pre * sigmoid_gate
    hidden = (silu_gate * up_pre).astype(jnp.bfloat16)
    gate_delta = (
        hidden_grad * up_pre * sigmoid_gate * (1.0 + gate_pre * (1.0 - sigmoid_gate))
    ).astype(jnp.bfloat16)
    up_delta = (hidden_grad * silu_gate).astype(jnp.bfloat16)
    return hidden, gate_delta, up_delta


def shards(tokens, route_ids, route_weights, gate_weight, up_weight, down_weight, out_grad):
    expert_count = lax.axis_size("expert")
    tok_count, width = tokens.shape
    top_count = route_ids.shape[1]
    capacity = min(tok_count, tok_count * top_count // expert_count + tok_count // 16)
    weight_g, weight_u, weight_d = gate_weight[0], up_weight[0], down_weight[0]
    place, scale = slot_matrices(route_ids, route_weights, expert_count, capacity)
    chunks, start = [], 0
    for size in SLOT_CHUNKS:
        chunks.append(
            tuple(
                m[:, start : start + size].reshape(expert_count * size, tok_count)
                for m in (place, scale)
            )
        )
        start += size
    assert start == capacity
    sent = []
    for place_c, scale_c in chunks:
        sent.append(
            swap(
                jnp.concatenate(
                    [
                        dot_of(place_c, tokens, 1, 0).astype(jnp.bfloat16),
                        dot_of(scale_c, out_grad, 1, 0).astype(jnp.bfloat16),
                    ],
                    axis=1,
                )
            )
        )
    parts, after = [], None
    for got in sent:
        if after is not None and False:
            got, after = lax.optimization_barrier((got, after))
            parts[-1] = parts[-1][:3] + after
        rows, upstream = got[:, :width], got[:, width:]
        partial = (
            dot_of(rows, weight_g, 1, 0).astype(jnp.bfloat16),
            dot_of(rows, weight_u, 1, 0).astype(jnp.bfloat16),
            dot_of(upstream, weight_d, 1, 1).astype(jnp.bfloat16),
        )
        after = lax.psum(partial, "dp")
        parts.append((rows, upstream, None) + tuple(after))
    mixed = input_grad = gate_grad = up_grad = down_grad = 0.0
    for (place_c, scale_c), (rows, upstream, _, *summed) in zip(chunks, parts):
        hidden, gate_delta, up_delta = pointwise(*(v.astype(jnp.float32) for v in summed))
        produced = dot_of(hidden, weight_d, 1, 0).astype(jnp.bfloat16)
        back_rows = (
            dot_of(gate_delta, weight_g, 1, 1) + dot_of(up_delta, weight_u, 1, 1)
        ).astype(jnp.bfloat16)
        back = swap(jnp.concatenate([produced, back_rows], axis=1))
        mixed += dot_of(scale_c, back[:, :width], 0, 0)
        input_grad += dot_of(place_c, back[:, width:], 0, 0)
        gate_grad += dot_of(rows, gate_delta, 0, 0)
        up_grad += dot_of(rows, up_delta, 0, 0)
        down_grad += dot_of(hidden, upstream, 0, 0)
    return (
        mixed.astype(jnp.bfloat16),
        input_grad.astype(jnp.bfloat16),
        gate_grad[None],
        up_grad[None],
        down_grad[None],
    )


def solution(mesh):
    return jax.shard_map(
        shards,
        mesh=mesh,
        in_specs=(
            P("expert", "dp"),
            P("expert", None),
            P("expert", None),
            P("expert", "dp", None),
            P("expert", "dp", None),
            P("expert", None, "dp"),
            P("expert", "dp"),
        ),
        out_specs=(
            P("expert", "dp"),
            P("expert", "dp"),
            P("expert", "dp", None),
            P("expert", "dp", None),
            P("expert", None, "dp"),
        ),
        check_vma=False,
    )
```

time: 581 us -> 267 us (0.46)
  waiting for transfers between devices: 402 us -> 177 us
  local copies, waits for them, and re-layouts: 86.8 us -> 4.19 us
  blocking collectives: 52.7 us -> 29.9 us
  starting transfers between devices: 0.38 us -> 11.7 us
  matrix products: 14.3 us -> 21.4 us
    reduce_scatter x2 -> x0, waiting for transfers between devices: 200 us -> none  [the longest x1 106 us: shards(): lax.psum_scatter((weighted[safe_row] * present).astype(jnp.bfloat16), 'ex...]
    all_gather x2 -> x0, blocking collectives: 52.7 us -> none  [the longest x1 28.6 us: shards(): lax.all_gather(route_weights, 'expert', axis=0, tiled=True)]
    scatter x3 -> x0, local copies, waits for them, and re-layouts: 52.1 us -> none  [the longest x2 36.6 us: shards(): jnp.zeros((row_total, width), jnp.bfloat16).at[dest_row]]
    all_gather x2 -> x0, waiting for transfers between devices: 36.3 us -> none  [the longest x1 36.2 us: shards(): lax.all_gather(out_grad, 'expert', axis=0, tiled=True)]
    gather x2 -> x0, local copies, waits for them, and re-layouts: 32.3 us -> none  [the longest x1 16.2 us: shards(): weighted[safe_row] * present]
    all_to_all x0 -> x1, blocking collectives: none -> 29.9 us  [swap(): lax.all_to_all(rows, 'expert', split_axis=0, concat_axis=0, tiled=True)]
    all_to_all x0 -> x1, waiting for transfers between devices: none -> 13.2 us  [swap(): lax.all_to_all(rows, 'expert', split_axis=0, concat_axis=0, tiled=True)]
    all_to_all x0 -> x1, starting transfers between devices: none -> 11.7 us  [swap(): lax.all_to_all(rows, 'expert', split_axis=0, concat_axis=0, tiled=True)]
  transfers between devices with their start and end apart: 5 -> 2, of which waited for: 4 -> 2; matrix products, arithmetic and copies ran while one was open for 8% -> 2% of each run, Pallas kernels for 0% -> 0%
where the time goes in v1:
time: 267 us; the launch traced here: 266 us
  waiting for transfers between devices  177 us (66%)
  blocking collectives  29.9 us (11%)
  matrix products  21.4 us (8%)
  between operations  14.2 us (5%)
  starting transfers between devices  11.7 us (4%)
  other arithmetic  8.11 us (3%)
  local copies, waits for them, and re-layouts  4.19 us (2%)
    psum x1, waiting for transfers between devices, shards(): after = lax.psum(partial, 'dp')  164 us
    all_to_all x1, blocking collectives, swap(): lax.all_to_all(rows, 'expert', split_axis=0, concat_axis=0, tiled=True)  29.9 us
    dot_general x14, matrix products, dot_of(): lax.dot_general(first_op, second_op, (((first_dim,), (second_dim,)), ((),...  21.4 us
    all_to_all x1, waiting for transfers between devices, swap(): lax.all_to_all(rows, 'expert', split_axis=0, concat_axis=0, tiled=True)  13.2 us
    all_to_all x1, starting transfers between devices, swap(): lax.all_to_all(rows, 'expert', split_axis=0, concat_axis=0, tiled=True)  11.7 us
  transfers between devices with their start and end apart: 2, of which 2 were waited for; matrix products, arithmetic and copies ran while one was open for 2% of the time, Pallas kernels for 0%

profile of v1, /device:TPU:1, one launch (start us, length us, event | category | flops | bytes accessed | tf_op | source)
XLA Modules:
  0.0 266.5 jit_solution(16248612039432697903)
XLA Ops:
  7.2 0.0 all-reduce.3.cloned.1.call-start
  7.2 0.8 fusion.29
  8.0 0.7 convert_bitcast_fusion
  8.7 0.7 select_reduce_fusion
  9.4 0.1 fusion.10
  9.6 0.1 iota.31
  9.7 0.2 fusion.15
  9.9 0.2 fusion.13
  10.2 1.2 convolution_convert_fusion.5
  11.4 1.2 convolution_convert_fusion.4
  12.6 0.1 pad_maximum_fusion
  12.7 0.7 copy.14
  13.4 29.9 %all_to_all.24 = bf16[32,40,512]{2,1,0:T(8,128)(2,1)S(1)} all-to-all(bf16[32,40,512]{2,1,0:T(8,128)(2,1)S(1)} %bitcast.60), channel_id=1, replica_groups=mesh['dp'=16,'expert'=32] {'expert'}, dimensions={0} | all-to-all | bytes 2621440 | tf_op jit(solution)/shard_map/all_to_all | solution.py:37
  43.3 2.0 convolution_convert_fusion.1
  45.3 2.1 convolution_convert_fusion
  47.3 2.0 convolution_convert_fusion.2
  49.3 163.7 %all-reduce.3.cloned.1.call-done = (bf16[1280,768]{1,0:T(8,128)(2,1)}, bf16[1280,768]{1,0:T(8,128)(2,1)}, bf16[1280,768]{1,0:T(8,128)(2,1)}) async-done(((bf16[1280,768]{1,0:T(8,128)(2,1)}, bf16[1280,768]{1,0:T(8,128)(2,1)}, bf16[1280,768]{1,0:T(8,128)(2,1)}), (bf16[1280,768]{1,0:T(8,128)(2,1)}, bf16[1280,768]{1,0:T(8,128)(2,1)}, bf16[1280,768]{1,0:T(8,128)(2,1)})) %all-reduce.3.cloned.1.call-update) | async-done | bytes 5898256 | tf_op jit(solution)/shard_map/psum | solution.py:92
  213.0 4.2 %fusion = (bf16[1280,768]{1,0:T(8,128)(2,1)S(1)}, bf16[1280,768]{1,0:T(8,128)(2,1)S(1)}, bf16[1280,768]{1,0:T(8,128)(2,1)S(1)}) fusion(bf16[1280,768]{1,0:T(8,128)(2,1)} %get-tuple-element.5, bf16[1280,768]{1,0:T(8,128)(2,1)} %get-tuple-element.7, bf16[1280,768]{1,0:T(8,128)(2,1)} %get-tuple-element.6), kind=kLoop, calls=%fused_computation.6 | loop fusion | flops 17694720 | bytes 11796480 | tf_op jit(solution)/shard_map/convert_element_type | solution.py:43
  217.3 0.7 convolution_convert_fusion.3
  218.0 0.6 copy-done.11
  218.6 0.7 fusion.26
  219.3 0.4 copy-done.9
  219.7 0.7 fusion.9
  220.5 1.1 pad_maximum_fusion.1
  221.6 2.4 copy.15
  224.0 11.7 %all-to-all-start.1 = ((bf16[32,40,512]{2,1,0:T(8,128)(2,1)}), bf16[32,40,512]{2,1,0:T(8,128)(2,1)}, u32[]{:S(2)}, u32[]{:S(2)}) async-start(bf16[32,40,512]{2,1,0:T(8,128)(2,1)} %bitcast.59), calls=%async_computation.1 | async-start | bytes 2621440 | tf_op jit(solution)/shard_map/all_to_all | solution.py:37
  235.7 3.4 %convolution_bitcast_fusion.2 = f32[1,256,768]{2,1,0:T(8,128)} fusion(bf16[1280,768]{1,0:T(8,128)(2,1)} %copy-done.1, bf16[1280,512]{1,0:T(8,128)(2,1)} %bitcast.56), kind=kOutput, calls=%fused_computation.27 | convolution fusion | flops 503316480 | bytes 3407872 | tf_op jit(solution)/shard_map/dot_general | solution.py:10
  239.2 1.6 convolution_bitcast_fusion.1
  240.8 1.6 convolution_bitcast_fusion
  242.4 13.2 %all-to-all-done.1 = bf16[32,40,512]{2,1,0:T(8,128)(2,1)} async-done(((bf16[32,40,512]{2,1,0:T(8,128)(2,1)}), bf16[32,40,512]{2,1,0:T(8,128)(2,1)}, u32[]{:S(2)}, u32[]{:S(2)}) %all-to-all-start.1) | async-done | bytes 1310752 | tf_op jit(solution)/shard_map/all_to_all | solution.py:37
  255.6 2.0 convolution_convert_fusion.6
  257.6 2.0 convolution_convert_fusion.7
  (24 shorter events, 0.1 us)
Async XLA Ops:
  7.2 38.1 %copy-start = (bf16[1,768,256]{2,1,0:T(8,128)(2,1)S(1)}, bf16[1,768,256]{2,1,0:T(8,128)(2,1)}, u32[]{:S(2)}) copy-start(bf16[1,768,256]{2,1,0:T(8,128)(2,1)} %param.12) | copy-start | bytes 1179652
  7.2 205.9 %all-reduce.3.cloned.1.call-start = ((), (), s32[]{:S(2)}) async-start(), calls=%async_computation.2 | async-start | bytes 11796480 | tf_op jit(solution)/shard_map/psum | solution.py:92
  9.9 1.5 copy-start.4
  13.4 29.9 %copy-start.8 = (bf16[1,256,768]{2,1,0:T(8,128)(2,1)S(1)}, bf16[1,256,768]{2,1,0:T(8,128)(2,1)}, u32[]{:S(2)}) copy-start(bf16[1,256,768]{2,1,0:T(8,128)(2,1)} %param.11) | copy-start | bytes 1179652
  43.3 4.0 %copy-start.2 = (bf16[32,40,512]{2,1,0:T(8,128)(2,1)}, bf16[32,40,512]{2,1,0:T(8,128)(2,1)S(1)}, u32[]{:S(2)}) copy-start(bf16[32,40,512]{2,1,0:T(8,128)(2,1)S(1)} %all_to_all.24) | copy-start | bytes 3932164
  45.3 2.1 copy-start.10
  217.3 2.0 copy-start.1
  217.3 2.0 copy-start.6
  217.3 1.3 copy-start.11
  218.6 1.1 copy-start.9
  224.0 31.6 %all-to-all-start.1 = ((bf16[32,40,512]{2,1,0:T(8,128)(2,1)}), bf16[32,40,512]{2,1,0:T(8,128)(2,1)}, u32[]{:S(2)}, u32[]{:S(2)}) async-start(bf16[32,40,512]{2,1,0:T(8,128)(2,1)} %bitcast.59), calls=%async_computation.1 | async-start | bytes 2621440 | tf_op jit(solution)/shard_map/all_to_all | solution.py:37
  235.7 3.4 %copy-start.3 = (bf16[32,40,512]{2,1,0:T(8,128)(2,1)S(1)}, bf16[32,40,512]{2,1,0:T(8,128)(2,1)}, u32[]{:S(2)}) copy-start(bf16[32,40,512]{2,1,0:T(8,128)(2,1)} %copy-done.2) | copy-start | bytes 3932164
  239.2 1.6 copy-start.7
  240.8 14.8 %copy-start.5 = (bf16[1280,128]{1,0:T(8,128)(2,1)S(1)}, bf16[1280,128]{1,0:T(8,128)(2,1)}, u32[]{:S(2)}) copy-start(bf16[1280,128]{1,0:T(8,128)(2,1)} %copy-done.4) | copy-start | bytes 983044
Sparse Core Ops, SparseCore 0:
  49.4 163.5 all-reduce.2

commit v2 on v1

--- a/solution.py
+++ b/solution.py
@@ -1,6 +1,10 @@
+import functools
+
 import jax
 import jax.numpy as jnp
 from jax import lax
+from jax.experimental import pallas as pl
+from jax.experimental.pallas import tpu as pltpu
 from jax.sharding import PartitionSpec as P
 
 SLOT_CHUNKS = (40,)
@@ -48,6 +52,132 @@
     return hidden, gate_delta, up_delta
 
 
+def ring_kernel(ring, *refs):
+    partials, outs = refs[:3], refs[3:6]
+    landed, sum_send, sum_recv, own_send, own_recv = refs[6:]
+    rows, units = partials[0].shape[0] // ring, partials[0].shape[1]
+    half = units // 2
+    me = lax.axis_index("dp")
+    peers = (lax.rem(me + 1, ring), lax.rem(me + ring - 1, ring))
+    streams = [(way, a) for a in range(3) for way in range(2)]
+
+    def block(ref, index, way):
+        at = lax.rem(index + 2 * ring, ring)
+        return ref.at[pl.ds(pl.multiple_of(at * rows, rows), rows), pl.ds(way * half, half)]
+
+    def dest(step, way):
+        return me - 1 - step if way == 0 else me + 1 + step
+
+    def sum_copy(step, way, a, first=False):
+        k = 2 * a + way
+        source = block(partials[a], dest(0, way), way) if first else landed.at[step - 1, k]
+        return pltpu.make_async_remote_copy(
+            src_ref=source,
+            dst_ref=landed.at[step, k],
+            send_sem=sum_send.at[step, k],
+            recv_sem=sum_recv.at[step, k],
+            device_id={"dp": peers[way]},
+            device_id_type=pl.DeviceIdType.MESH,
+        )
+
+    def own_copy(step, way, a):
+        k = 2 * a + way
+        place = block(outs[a], me - step if way == 0 else me + step, way)
+        return pltpu.make_async_remote_copy(
+            src_ref=place,
+            dst_ref=place,
+            send_sem=own_send.at[step, k],
+            recv_sem=own_recv.at[step, k],
+            device_id={"dp": peers[way]},
+            device_id_type=pl.DeviceIdType.MESH,
+        )
+
+    def own_arrival(step, way, a):
+        k = 2 * a + way
+        place = block(outs[a], me - 1 - step if way == 0 else me + 1 + step, way)
+        return pltpu.make_async_remote_copy(
+            src_ref=place,
+            dst_ref=place,
+            send_sem=own_send.at[step, k],
+            recv_sem=own_recv.at[step, k],
+            device_id={"dp": peers[way]},
+            device_id_type=pl.DeviceIdType.MESH,
+        )
+
+    def total(step, way, a):
+        mine = block(partials[a], dest(step + 1, way), way)[...].astype(jnp.float32)
+        return landed[step, 2 * a + way].astype(jnp.float32) + mine
+
+    barrier = pltpu.get_barrier_semaphore()
+    for peer in peers:
+        pl.semaphore_signal(
+            barrier, inc=1, device_id={"dp": peer}, device_id_type=pl.DeviceIdType.MESH
+        )
+    pl.semaphore_wait(barrier, 2)
+
+    for way, a in streams:
+        sum_copy(0, way, a, True).start()
+
+    def sum_step(step, carry):
+        for way, a in streams:
+            sum_copy(step, way, a, True).wait_recv()
+            landed[step, 2 * a + way] = total(step, way, a).astype(jnp.bfloat16)
+            sum_copy(step + 1, way, a).start()
+        return carry
+
+    lax.fori_loop(0, ring - 2, sum_step, 0)
+
+    last = ring - 2
+    for way in range(2):
+        for a in range(3):
+            sum_copy(last, way, a, True).wait_recv()
+        values = pointwise(*(total(last, way, a) for a in range(3)))
+        for a in range(3):
+            block(outs[a], me, way)[...] = values[a]
+        for a in range(3):
+            own_copy(0, way, a).start()
+
+    def own_step(step, carry):
+        for way, a in streams:
+            own_arrival(step, way, a).wait_recv()
+            own_copy(step + 1, way, a).start()
+        return carry
+
+    lax.fori_loop(0, ring - 2, own_step, 0)
+    for way, a in streams:
+        own_arrival(last, way, a).wait_recv()
+
+    def drain(step, carry):
+        for way, a in streams:
+            sum_copy(step, way, a, True).wait_send()
+            own_copy(step, way, a).wait_send()
+        return carry
+
+    lax.fori_loop(0, ring - 1, drain, 0)
+
+
+def reduced_units(partials):
+    ring = lax.axis_size("dp")
+    rows, units = partials[0].shape
+    sems = pltpu.SemaphoreType.DMA((ring - 1, 6))
+    return pl.pallas_call(
+        functools.partial(ring_kernel, ring),
+        out_shape=[jax.ShapeDtypeStruct((rows, units), jnp.bfloat16)] * 3,
+        in_specs=[pl.BlockSpec(memory_space=pltpu.VMEM)] * 3,
+        out_specs=[pl.BlockSpec(memory_space=pltpu.VMEM)] * 3,
+        scratch_shapes=[
+            pltpu.VMEM((ring - 1, 6, rows // ring, units // 2), jnp.bfloat16),
+            sems,
+            sems,
+            sems,
+            sems,
+        ],
+        compiler_params=pltpu.CompilerParams(
+            collective_id=0, has_side_effects=True, vmem_limit_bytes=48 * 1024 * 1024
+        ),
+    )(*partials)
+
+
 def shards(tokens, route_ids, route_weights, gate_weight, up_weight, down_weight, out_grad):
     expert_count = lax.axis_size("expert")
     tok_count, width = tokens.shape
@@ -89,11 +219,11 @@
             dot_of(rows, weight_u, 1, 0).astype(jnp.bfloat16),
             dot_of(upstream, weight_d, 1, 1).astype(jnp.bfloat16),
         )
-        after = lax.psum(partial, "dp")
+        after = reduced_units(partial)
         parts.append((rows, upstream, None) + tuple(after))
     mixed = input_grad = gate_grad = up_grad = down_grad = 0.0
     for (place_c, scale_c), (rows, upstream, _, *summed) in zip(chunks, parts):
-        hidden, gate_delta, up_delta = pointwise(*(v.astype(jnp.float32) for v in summed))
+        hidden, gate_delta, up_delta = summed
         produced = dot_of(hidden, weight_d, 1, 0).astype(jnp.bfloat16)
         back_rows = (
             dot_of(gate_delta, weight_g, 1, 1) + dot_of(up_delta, weight_u, 1, 1)

time: 267 us -> 217 us (0.81)
  waiting for transfers between devices: 177 us -> 13.3 us
  Pallas kernels: 0 us -> 135 us
  between operations: 14.2 us -> 0.8 us
  other arithmetic: 8.11 us -> 3.93 us
  starting transfers between devices: 11.7 us -> 8.58 us
    psum x1 -> x0, waiting for transfers between devices: 164 us -> none  [shards(): after = lax.psum(partial, 'dp')]
    pallas_call x0 -> x1, Pallas kernels: none -> 135 us  [reduced_units(): pl.pallas_call(functools.partial(ring_kernel, ring), out_shape=[jax.Shape...]
    convert_element_type x1 -> x0, other arithmetic: 4.22 us -> none  [pointwise(): hidden = (silu_gate * up_pre).astype(jnp.bfloat16)]
    all_to_all x1, starting transfers between devices: 11.7 us -> 8.58 us  [swap(): lax.all_to_all(rows, 'expert', split_axis=0, concat_axis=0, tiled=True)]
  transfers between devices with their start and end apart: 2 -> 1, of which waited for: 2 -> 1; matrix products, arithmetic and copies ran while one was open for 2% -> 3% of each run, Pallas kernels for 0% -> 0%
where the time goes in v2:
time: 217 us; the launch traced here: 216 us
  Pallas kernels  135 us (62%)
  blocking collectives  29.9 us (14%)
  matrix products  21.3 us (10%)
  waiting for transfers between devices  13.3 us (6%)
  starting transfers between devices  8.58 us (4%)
  other arithmetic  3.93 us (2%)
  local copies, waits for them, and re-layouts  3.67 us (2%)
    pallas_call x1, Pallas kernels, reduced_units(): pl.pallas_call(functools.partial(ring_kernel, ring), out_shape=[jax.Shape...  135 us
    all_to_all x1, blocking collectives, swap(): lax.all_to_all(rows, 'expert', split_axis=0, concat_axis=0, tiled=True)  29.9 us
    dot_general x14, matrix products, dot_of(): lax.dot_general(first_op, second_op, (((first_dim,), (second_dim,)), ((),...  21.3 us
    all_to_all x1, waiting for transfers between devices, swap(): lax.all_to_all(rows, 'expert', split_axis=0, concat_axis=0, tiled=True)  13.3 us
    all_to_all x1, starting transfers between devices, swap(): lax.all_to_all(rows, 'expert', split_axis=0, concat_axis=0, tiled=True)  8.58 us
  transfers between devices with their start and end apart: 1, of which 1 were waited for; matrix products, arithmetic and copies ran while one was open for 3% of the time, Pallas kernels for 0%

profile of v2, /device:TPU:1, one launch (start us, length us, event | category | flops | bytes accessed | tf_op | source)
XLA Modules:
  0.0 216.3 jit_solution(5728619801767705677)
XLA Ops:
  0.6 0.0 copy-start
  0.6 0.8 fusion.20
  1.4 0.7 convert_bitcast_fusion
  2.1 0.7 select_reduce_fusion
  2.9 0.1 fusion.1
  3.0 0.1 iota.31
  3.1 0.2 fusion.6
  3.3 0.0 copy-start.6
  3.3 0.2 fusion.4
  3.6 1.2 convolution_convert_fusion.5
  4.8 1.2 convolution_convert_fusion.4
  6.0 0.1 pad_maximum_fusion
  6.1 0.7 copy.14
  6.8 0.0 copy-start.8
  6.8 29.9 %all_to_all.24 = bf16[32,40,512]{2,1,0:T(8,128)(2,1)S(1)} all-to-all(bf16[32,40,512]{2,1,0:T(8,128)(2,1)S(1)} %bitcast.60), channel_id=1, replica_groups=mesh['dp'=16,'expert'=32] {'expert'}, dimensions={0} | all-to-all | bytes 2621440 | tf_op jit(solution)/shard_map/all_to_all | solution.py:41
  36.7 2.0 convolution_convert_fusion.1.refs_1_
  38.7 2.0 convolution_convert_fusion.refs_2_
  40.7 1.9 convolution_convert_fusion.2.refs_0_
  42.7 134.8 %shard_map.110 = (bf16[1280,768]{1,0:T(8,128)(2,1)S(1)}, bf16[1280,768]{1,0:T(8,128)(2,1)S(1)}, bf16[1280,768]{1,0:T(8,128)(2,1)S(1)}) custom-call(bf16[1280,768]{1,0:T(8,128)(2,1)} %convolution_convert_fusion.2.refs_0_, bf16[1280,768]{1,0:T(8,128)(2,1)} %convolution_convert_fusion.1.refs_1_, bf16[1280,768]{1,0:T(8,128)(2,1)} %convolution_convert_fusion.refs_2_), custom_call_target="tpu_custom_call" | custom-call | tf_op jit(solution)/shard_map/pallas_call | solution.py:163
  177.5 0.7 convolution_convert_fusion.3
  178.2 0.7 fusion.17
  179.0 0.4 copy-done.2
  179.4 0.7 fusion
  180.1 1.2 pad_maximum_fusion.1
  181.3 2.4 %copy.15 = bf16[1280,512]{1,0:T(8,128)(2,1)} copy(bf16[1280,512]{0,1:T(8,128)(2,1)} %pad_maximum_fusion.1) | data formatting | bytes 2621440 | tf_op jit(solution)/shard_map/concatenate | solution.py:231
  183.7 8.6 %all-to-all-start.1 = ((bf16[32,40,512]{2,1,0:T(8,128)(2,1)}), bf16[32,40,512]{2,1,0:T(8,128)(2,1)}, u32[]{:S(2)}, u32[]{:S(2)}) async-start(bf16[32,40,512]{2,1,0:T(8,128)(2,1)} %bitcast.59), calls=%async_computation.1 | async-start | bytes 2621440 | tf_op jit(solution)/shard_map/all_to_all | solution.py:41
  192.3 3.4 %convolution_bitcast_fusion.2 = f32[1,256,768]{2,1,0:T(8,128)} fusion(bf16[1280,768]{1,0:T(8,128)(2,1)} %copy-done.1, bf16[1280,512]{1,0:T(8,128)(2,1)} %bitcast.56), kind=kOutput, calls=%fused_computation.12 | convolution fusion | flops 503316480 | bytes 3407872 | tf_op jit(solution)/shard_map/dot_general | solution.py:14
  195.8 1.6 convolution_bitcast_fusion.1
  197.4 1.6 convolution_bitcast_fusion
  199.0 13.3 %all-to-all-done.1 = bf16[32,40,512]{2,1,0:T(8,128)(2,1)} async-done(((bf16[32,40,512]{2,1,0:T(8,128)(2,1)}), bf16[32,40,512]{2,1,0:T(8,128)(2,1)}, u32[]{:S(2)}, u32[]{:S(2)}) %all-to-all-start.1) | async-done | bytes 1310752 | tf_op jit(solution)/shard_map/all_to_all | solution.py:41
  212.3 2.0 convolution_convert_fusion.6
  214.3 2.0 convolution_convert_fusion.7
  (17 shorter events, 0.0 us)
Async XLA Ops:
  0.6 38.1 %copy-start = (bf16[1,768,256]{2,1,0:T(8,128)(2,1)S(1)}, bf16[1,768,256]{2,1,0:T(8,128)(2,1)}, u32[]{:S(2)}) copy-start(bf16[1,768,256]{2,1,0:T(8,128)(2,1)} %param.12) | copy-start | bytes 1179652
  3.3 1.5 copy-start.6
  6.8 29.9 %copy-start.8 = (bf16[1,256,768]{2,1,0:T(8,128)(2,1)S(1)}, bf16[1,256,768]{2,1,0:T(8,128)(2,1)}, u32[]{:S(2)}) copy-start(bf16[1,256,768]{2,1,0:T(8,128)(2,1)} %param.11) | copy-start | bytes 1179652
  36.7 4.0 %copy-start.4 = (bf16[32,40,512]{2,1,0:T(8,128)(2,1)}, bf16[32,40,512]{2,1,0:T(8,128)(2,1)S(1)}, u32[]{:S(2)}) copy-start(bf16[32,40,512]{2,1,0:T(8,128)(2,1)S(1)} %all_to_all.24) | copy-start | bytes 3932164
  38.7 2.0 copy-start.9
  177.5 1.5 copy-start.1
  177.5 1.9 copy-start.2
  183.7 28.5 %all-to-all-start.1 = ((bf16[32,40,512]{2,1,0:T(8,128)(2,1)}), bf16[32,40,512]{2,1,0:T(8,128)(2,1)}, u32[]{:S(2)}, u32[]{:S(2)}) async-start(bf16[32,40,512]{2,1,0:T(8,128)(2,1)} %bitcast.59), calls=%async_computation.1 | async-start | bytes 2621440 | tf_op jit(solution)/shard_map/all_to_all | solution.py:41
  192.3 3.4 %copy-start.5 = (bf16[32,40,512]{2,1,0:T(8,128)(2,1)S(1)}, bf16[32,40,512]{2,1,0:T(8,128)(2,1)}, u32[]{:S(2)}) copy-start(bf16[32,40,512]{2,1,0:T(8,128)(2,1)} %copy-done.4) | copy-start | bytes 3932164
  195.8 1.6 copy-start.3
  197.4 14.9 %copy-start.7 = (bf16[1280,128]{1,0:T(8,128)(2,1)S(1)}, bf16[1280,128]{1,0:T(8,128)(2,1)}, u32[]{:S(2)}) copy-start(bf16[1280,128]{1,0:T(8,128)(2,1)} %copy-done.6) | copy-start | bytes 983044

commit v3 on v2

--- a/solution.py
+++ b/solution.py
@@ -7,7 +7,7 @@
 from jax.experimental.pallas import tpu as pltpu
 from jax.sharding import PartitionSpec as P
 
-SLOT_CHUNKS = (40,)
+SLOT_CHUNKS = (24, 16)
 
 
 def dot_of(first_op, second_op, first_dim, second_dim):
@@ -156,7 +156,7 @@
     lax.fori_loop(0, ring - 1, drain, 0)
 
 
-def reduced_units(partials):
+def reduced_units(partials, number):
     ring = lax.axis_size("dp")
     rows, units = partials[0].shape
     sems = pltpu.SemaphoreType.DMA((ring - 1, 6))
@@ -173,7 +173,10 @@
             sems,
         ],
         compiler_params=pltpu.CompilerParams(
-            collective_id=0, has_side_effects=True, vmem_limit_bytes=48 * 1024 * 1024
+            collective_id=number, has_side_effects=True, vmem_limit_bytes=48 * 1024 * 1024
+        ),
+        cost_estimate=pl.CostEstimate(
+            flops=40 * rows * units, bytes_accessed=300_000_000, transcendentals=0
         ),
     )(*partials)
 
@@ -208,29 +211,33 @@
                 )
             )
         )
-    parts, after = [], None
-    for got in sent:
-        if after is not None and False:
-            got, after = lax.optimization_barrier((got, after))
-            parts[-1] = parts[-1][:3] + after
+    mixed = input_grad = gate_grad = up_grad = down_grad = 0.0
+    out = None
+    backs, kept = [], []
+    for number, got in enumerate(sent):
+        if out is not None:
+            got, out = lax.optimization_barrier((got, out))
+            backs.append(swap(out))
         rows, upstream = got[:, :width], got[:, width:]
-        partial = (
-            dot_of(rows, weight_g, 1, 0).astype(jnp.bfloat16),
-            dot_of(rows, weight_u, 1, 0).astype(jnp.bfloat16),
-            dot_of(upstream, weight_d, 1, 1).astype(jnp.bfloat16),
-        )
-        after = reduced_units(partial)
-        parts.append((rows, upstream, None) + tuple(after))
-    mixed = input_grad = gate_grad = up_grad = down_grad = 0.0
-    for (place_c, scale_c), (rows, upstream, _, *summed) in zip(chunks, parts):
-        hidden, gate_delta, up_delta = summed
+        hidden, gate_delta, up_delta = reduced_units(
+            (
+                dot_of(rows, weight_g, 1, 0).astype(jnp.bfloat16),
+                dot_of(rows, weight_u, 1, 0).astype(jnp.bfloat16),
+                dot_of(upstream, weight_d, 1, 1).astype(jnp.bfloat16),
+            ),
+            number,
+        )
         produced = dot_of(hidden, weight_d, 1, 0).astype(jnp.bfloat16)
         back_rows = (
             dot_of(gate_delta, weight_g, 1, 1) + dot_of(up_delta, weight_u, 1, 1)
         ).astype(jnp.bfloat16)
-        back = swap(jnp.concatenate([produced, back_rows], axis=1))
+        out = jnp.concatenate([produced, back_rows], axis=1)
+        kept.append((rows, upstream, hidden, gate_delta, up_delta))
+    backs.append(swap(out))
+    for (place_c, scale_c), back in zip(chunks, backs):
         mixed += dot_of(scale_c, back[:, :width], 0, 0)
         input_grad += dot_of(place_c, back[:, width:], 0, 0)
+    for rows, upstream, hidden, gate_delta, up_delta in kept:
         gate_grad += dot_of(rows, gate_delta, 0, 0)
         up_grad += dot_of(rows, up_delta, 0, 0)
         down_grad += dot_of(hidden, upstream, 0, 0)

time: 217 us -> 312 us (1.44)
  starting transfers between devices: 8.58 us -> 69.3 us
  Pallas kernels: 135 us -> 179 us
  blocking collectives: 29.9 us -> 0 us
  local copies, waits for them, and re-layouts: 3.67 us -> 11.3 us
  waiting for transfers between devices: 13.3 us -> 20.1 us
  matrix products: 21.3 us -> 26.2 us
    all_to_all x1 -> x4, starting transfers between devices: 8.58 us -> 69.3 us  [swap(): lax.all_to_all(rows, 'expert', split_axis=0, concat_axis=0, tiled=True)]
    pallas_call x1 -> x2, Pallas kernels: 135 us -> 179 us  [reduced_units(): pl.pallas_call(functools.partial(ring_kernel, ring), out_shape=[jax.Shape...]
    all_to_all x1 -> x0, blocking collectives: 29.9 us -> none  [swap(): lax.all_to_all(rows, 'expert', split_axis=0, concat_axis=0, tiled=True)]
    all_to_all x1 -> x4, waiting for transfers between devices: 13.3 us -> 20.1 us  [swap(): lax.all_to_all(rows, 'expert', split_axis=0, concat_axis=0, tiled=True)]
    unnamed x20 -> x56, local copies, waits for them, and re-layouts: 0.49 us -> 5.91 us
    dot_general x14 -> x27, matrix products: 21.3 us -> 26.2 us  [dot_of(): lax.dot_general(first_op, second_op, (((first_dim,), (second_dim,)), ((),...]
  transfers between devices with their start and end apart: 1 -> 4, of which waited for: 1 -> 2; matrix products, arithmetic and copies ran while one was open for 3% -> 7% of each run, Pallas kernels for 0% -> 57%
where the time goes in v3:
time: 312 us; the launch traced here: 311 us
  Pallas kernels  179 us (57%)
  starting transfers between devices  69.3 us (22%)
  matrix products  26.2 us (8%)
  waiting for transfers between devices  20.1 us (6%)
  local copies, waits for them, and re-layouts  11.3 us (4%)
  other arithmetic  4.22 us (1%)
    pallas_call x2, Pallas kernels, reduced_units(): pl.pallas_call(functools.partial(ring_kernel, ring), out_shape=[jax.Shape...  179 us
    all_to_all x4, starting transfers between devices, swap(): lax.all_to_all(rows, 'expert', split_axis=0, concat_axis=0, tiled=True)  69.3 us
    dot_general x27, matrix products, dot_of(): lax.dot_general(first_op, second_op, (((first_dim,), (second_dim,)), ((),...  26.2 us
    all_to_all x4, waiting for transfers between devices, swap(): lax.all_to_all(rows, 'expert', split_axis=0, concat_axis=0, tiled=True)  20.1 us
  transfers between devices with their start and end apart: 4, of which 2 were waited for; matrix products, arithmetic and copies ran while one was open for 7% of the time, Pallas kernels for 57%

profile of v3, /device:TPU:1, one launch (start us, length us, event | category | flops | bytes accessed | tf_op | source)
XLA Modules:
  0.0 311.1 jit_solution(9861865467595478044)
XLA Ops:
  0.7 0.8 fusion.43
  4.4 1.2 copy.17
  5.5 10.4 %all-to-all-start.1 = ((bf16[32,24,512]{2,1,0:T(8,128)(2,1)}), bf16[32,24,512]{2,1,0:T(8,128)(2,1)S(1)}, u32[]{:S(2)}, u32[]{:S(2)}) async-start(bf16[32,24,512]{2,1,0:T(8,128)(2,1)} %bitcast.8), calls=%async_computation.1 | async-start | bytes 1572864 | tf_op jit(solution)/shard_map/all_to_all | solution.py:41
  17.0 1.0 copy.16
  18.0 12.3 %all-to-all-done.1 = bf16[32,24,512]{2,1,0:T(8,128)(2,1)S(1)} async-done(((bf16[32,24,512]{2,1,0:T(8,128)(2,1)}), bf16[32,24,512]{2,1,0:T(8,128)(2,1)S(1)}, u32[]{:S(2)}, u32[]{:S(2)}) %all-to-all-start.1) | async-done | bytes 786464 | tf_op jit(solution)/shard_map/all_to_all | solution.py:41
  30.3 3.8 %all-to-all-start = ((bf16[32,16,512]{2,1,0:T(8,128)(2,1)}), bf16[32,16,512]{2,1,0:T(8,128)(2,1)S(1)}, u32[]{:S(2)}, u32[]{:S(2)}) async-start(bf16[32,16,512]{2,1,0:T(8,128)(2,1)} %bitcast.5), calls=%async_computation | async-start | bytes 1048576 | tf_op jit(solution)/shard_map/all_to_all | solution.py:41
  34.5 1.5 convolution_convert_fusion.refs_2_
  36.5 97.1 %shard_map.110 = (bf16[768,768]{1,0:T(8,128)(2,1)S(1)}, bf16[768,768]{1,0:T(8,128)(2,1)S(1)}, bf16[768,768]{1,0:T(8,128)(2,1)S(1)}) custom-call(bf16[768,768]{1,0:T(8,128)(2,1)S(1)} %convolution_convert_fusion.2.refs_0_, bf16[768,768]{1,0:T(8,128)(2,1)S(1)} %convolution_convert_fusion.1.refs_1_, bf16[768,768]{1,0:T(8,128)(2,1)} %convolution_convert_fusion.refs_2_), custom_call_target="tpu_custom_call" | custom-call | flops 23592960 | bytes 300000000 | tf_op jit(solution)/shard_map/pallas_call | solution.py:163
  136.0 0.9 pad_maximum_fusion.1
  136.9 1.4 fusion.33
  138.3 2.5 convolution_convert_fusion.4.refs_1_
  140.8 1.3 convolution_convert_fusion.3.refs_2_
  142.1 1.2 convolution_convert_fusion.5.refs_0_
  143.4 1.2 copy.18
  144.6 27.2 %all-to-all-start.2 = ((bf16[32,24,512]{2,1,0:T(8,128)(2,1)}), bf16[32,24,512]{2,1,0:T(8,128)(2,1)}, u32[]{:S(2)}, u32[]{:S(2)}) async-start(bf16[32,24,512]{2,1,0:T(8,128)(2,1)} %bitcast.13), calls=%async_computation.2 | async-start | bytes 1572864 | tf_op jit(solution)/shard_map/all_to_all | solution.py:41
  171.8 1.1 copy-done.1
  172.9 1.1 copy-done.2
  174.1 1.1 copy-done.3
  175.2 81.7 %shard_map.111 = (bf16[512,768]{1,0:T(8,128)(2,1)S(1)}, bf16[512,768]{1,0:T(8,128)(2,1)S(1)}, bf16[512,768]{1,0:T(8,128)(2,1)S(1)}) custom-call(bf16[512,768]{1,0:T(8,128)(2,1)S(1)} %copy-done.3, bf16[512,768]{1,0:T(8,128)(2,1)S(1)} %copy-done.1, bf16[512,768]{1,0:T(8,128)(2,1)S(1)} %copy-done.2), custom_call_target="tpu_custom_call" | custom-call | flops 15728640 | bytes 300000000 | tf_op jit(solution)/shard_map/pallas_call | solution.py:163
  258.7 1.3 fusion.2
  260.3 0.8 pad_maximum_fusion.3
  261.2 2.1 copy.19
  263.2 1.9 fusion.26
  265.2 1.3 fusion
  266.5 1.4 fusion.31
  267.9 27.9 %all-to-all-start.3 = ((bf16[32,16,512]{2,1,0:T(8,128)(2,1)}), bf16[32,16,512]{2,1,0:T(8,128)(2,1)}, u32[]{:S(2)}, u32[]{:S(2)}) async-start(bf16[32,16,512]{2,1,0:T(8,128)(2,1)} %bitcast.85), calls=%async_computation.3 | async-start | bytes 1048576 | tf_op jit(solution)/shard_map/all_to_all | solution.py:41
  295.9 1.3 fusion.1
  297.1 1.3 fusion.8
  298.4 1.2 fusion.10
  299.7 7.8 %all-to-all-done.3 = bf16[32,16,512]{2,1,0:T(8,128)(2,1)} async-done(((bf16[32,16,512]{2,1,0:T(8,128)(2,1)}), bf16[32,16,512]{2,1,0:T(8,128)(2,1)}, u32[]{:S(2)}, u32[]{:S(2)}) %all-to-all-start.3) | async-done | bytes 524320 | tf_op jit(solution)/shard_map/all_to_all | solution.py:41
  307.5 1.8 fusion.6
  309.3 1.8 fusion.5
  (78 shorter events, 9.2 us)
Async XLA Ops:
  0.6 33.9 %copy-start = (bf16[1,768,256]{2,1,0:T(8,128)(2,1)S(1)}, bf16[1,768,256]{2,1,0:T(8,128)(2,1)}, u32[]{:S(2)}) copy-start(bf16[1,768,256]{2,1,0:T(8,128)(2,1)} %param.12) | copy-start | bytes 1179652
  0.6 2.6 copy-start.27
  0.7 3.3 %copy-start.26 = (bf16[128,256]{1,0:T(8,128)(2,1)S(1)}, bf16[128,256]{1,0:T(8,128)(2,1)}, u32[]{:S(2)}) copy-start(bf16[128,256]{1,0:T(8,128)(2,1)} %param.13) | copy-start | bytes 196612
  3.2 0.7 copy-start.18
  3.3 0.7 copy-start.20
  5.5 24.8 %all-to-all-start.1 = ((bf16[32,24,512]{2,1,0:T(8,128)(2,1)}), bf16[32,24,512]{2,1,0:T(8,128)(2,1)S(1)}, u32[]{:S(2)}, u32[]{:S(2)}) async-start(bf16[32,24,512]{2,1,0:T(8,128)(2,1)} %bitcast.8), calls=%async_computation.1 | async-start | bytes 1572864 | tf_op jit(solution)/shard_map/all_to_all | solution.py:41
  15.9 0.7 copy-start.22
  16.0 0.7 copy-start.24
  17.0 17.1 %copy-start.12 = (bf16[1,256,768]{2,1,0:T(8,128)(2,1)S(1)}, bf16[1,256,768]{2,1,0:T(8,128)(2,1)}, u32[]{:S(2)}) copy-start(bf16[1,256,768]{2,1,0:T(8,128)(2,1)} %param.11) | copy-start | bytes 1179652
  30.3 106.7 %copy-start.5 = (bf16[32,24,512]{2,1,0:T(8,128)(2,1)}, bf16[32,24,512]{2,1,0:T(8,128)(2,1)S(1)}, u32[]{:S(2)}) copy-start(bf16[32,24,512]{2,1,0:T(8,128)(2,1)S(1)} %all-to-all-done.1) | copy-start | bytes 2359300
  30.3 108.1 %all-to-all-start = ((bf16[32,16,512]{2,1,0:T(8,128)(2,1)}), bf16[32,16,512]{2,1,0:T(8,128)(2,1)S(1)}, u32[]{:S(2)}, u32[]{:S(2)}) async-start(bf16[32,16,512]{2,1,0:T(8,128)(2,1)} %bitcast.5), calls=%async_computation | async-start | bytes 1048576 | tf_op jit(solution)/shard_map/all_to_all | solution.py:41
  34.5 1.5 copy-start.11
  133.7 1.8 copy-start.4
  133.7 1.3 copy-start.13
  138.3 3.8 %copy-start.7 = (bf16[32,16,512]{2,1,0:T(8,128)(2,1)}, bf16[32,16,512]{2,1,0:T(8,128)(2,1)S(1)}, u32[]{:S(2)}) copy-start(bf16[32,16,512]{2,1,0:T(8,128)(2,1)S(1)} %all-to-all-done) | copy-start | bytes 1572868
  140.8 2.6 copy-start.15
  144.6 123.3 %all-to-all-start.2 = ((bf16[32,24,512]{2,1,0:T(8,128)(2,1)}), bf16[32,24,512]{2,1,0:T(8,128)(2,1)}, u32[]{:S(2)}, u32[]{:S(2)}) async-start(bf16[32,24,512]{2,1,0:T(8,128)(2,1)} %bitcast.13), calls=%async_computation.2 | async-start | bytes 1572864 | tf_op jit(solution)/shard_map/all_to_all | solution.py:41
  171.8 1.1 copy-start.1
  172.9 1.1 copy-start.2
  174.1 1.1 copy-start.3
  257.4 1.0 copy-start.8
  257.4 1.3 copy-start.16
  258.7 1.3 copy-start.14
  263.2 1.9 copy-start.9
  265.1 1.3 copy-start.6
  266.5 29.4 %copy-start.10 = (bf16[32,16,512]{2,1,0:T(8,128)(2,1)S(1)}, bf16[32,16,512]{2,1,0:T(8,128)(2,1)}, u32[]{:S(2)}) copy-start(bf16[32,16,512]{2,1,0:T(8,128)(2,1)} %copy-done.7) | copy-start | bytes 1572868
  267.9 28.0 %copy-start.17 = (f32[256,768]{1,0:T(8,128)S(1)}, f32[256,768]{1,0:T(8,128)}, u32[]{:S(2)}) copy-start(f32[256,768]{1,0:T(8,128)} %fusion.31) | copy-start | bytes 2359300
  267.9 39.6 %all-to-all-start.3 = ((bf16[32,16,512]{2,1,0:T(8,128)(2,1)}), bf16[32,16,512]{2,1,0:T(8,128)(2,1)}, u32[]{:S(2)}, u32[]{:S(2)}) async-start(bf16[32,16,512]{2,1,0:T(8,128)(2,1)} %bitcast.85), calls=%async_computation.3 | async-start | bytes 1048576 | tf_op jit(solution)/shard_map/all_to_all | solution.py:41
  295.8 1.3 copy-start.21
  295.9 2.6 copy-start.19
  297.1 10.3 %copy-start.25 = (bf16[32,16,128]{2,1,0:T(8,128)(2,1)S(1)}, bf16[32,16,128]{2,1,0:T(8,128)(2,1)}, u32[]{:S(2)}) copy-start(bf16[32,16,128]{2,1,0:T(8,128)(2,1)} %copy-done.24) | copy-start | bytes 393220
  297.1 12.1 %copy-start.23 = (bf16[32,16,128]{2,1,0:T(8,128)(2,1)S(1)}, bf16[32,16,128]{2,1,0:T(8,128)(2,1)}, u32[]{:S(2)}) copy-start(bf16[32,16,128]{2,1,0:T(8,128)(2,1)} %copy-done.22) | copy-start | bytes 393220

commit v4 on v2

--- a/solution.py
+++ b/solution.py
@@ -55,18 +55,18 @@
 def ring_kernel(ring, *refs):
     partials, outs = refs[:3], refs[3:6]
     landed, sum_send, sum_recv, own_send, own_recv = refs[6:]
-    rows, units = partials[0].shape[0] // ring, partials[0].shape[1]
-    half = units // 2
+    rows = partials[0].shape[0] // ring
+    hops = (ring // 2, ring - 1 - ring // 2)
     me = lax.axis_index("dp")
     peers = (lax.rem(me + 1, ring), lax.rem(me + ring - 1, ring))
     streams = [(way, a) for a in range(3) for way in range(2)]
 
     def block(ref, index, way):
         at = lax.rem(index + 2 * ring, ring)
-        return ref.at[pl.ds(pl.multiple_of(at * rows, rows), rows), pl.ds(way * half, half)]
+        return ref.at[pl.ds(pl.multiple_of(at * rows, rows), rows), :]
 
     def dest(step, way):
-        return me - 1 - step if way == 0 else me + 1 + step
+        return me + hops[0] - step if way == 0 else me - hops[1] + step
 
     def sum_copy(step, way, a, first=False):
         k = 2 * a + way
@@ -118,55 +118,59 @@
     for way, a in streams:
         sum_copy(0, way, a, True).start()
 
-    def sum_step(step, carry):
-        for way, a in streams:
-            sum_copy(step, way, a, True).wait_recv()
-            landed[step, 2 * a + way] = total(step, way, a).astype(jnp.bfloat16)
-            sum_copy(step + 1, way, a).start()
-        return carry
-
-    lax.fori_loop(0, ring - 2, sum_step, 0)
-
-    last = ring - 2
-    for way in range(2):
-        for a in range(3):
-            sum_copy(last, way, a, True).wait_recv()
-        values = pointwise(*(total(last, way, a) for a in range(3)))
-        for a in range(3):
-            block(outs[a], me, way)[...] = values[a]
-        for a in range(3):
-            own_copy(0, way, a).start()
-
-    def own_step(step, carry):
-        for way, a in streams:
-            own_arrival(step, way, a).wait_recv()
-            own_copy(step + 1, way, a).start()
-        return carry
-
-    lax.fori_loop(0, ring - 2, own_step, 0)
+    def sum_forward(step, way, a):
+        sum_copy(step, way, a, True).wait_recv()
+        landed[step, 2 * a + way] = total(step, way, a).astype(jnp.bfloat16)
+        sum_copy(step + 1, way, a).start()
+
+    def own_forward(step, way, a):
+        own_arrival(step, way, a).wait_recv()
+        own_copy(step + 1, way, a).start()
+
+    def drain(step, way, a):
+        sum_copy(step, way, a, True).wait_send()
+        own_copy(step, way, a).wait_send()
+
+    def run(act, less):
+        def both(step, carry):
+            for way, a in streams:
+                act(step, way, a)
+            return carry
+
+        lax.fori_loop(0, hops[1] - less, both, 0)
+        for step in range(hops[1] - less, hops[0] - less):
+            for a in range(3):
+                act(step, 0, a)
+
+    run(sum_forward, 1)
+    values = []
+    for a in range(3):
+        sum_copy(hops[0] - 1, 0, a, True).wait_recv()
+        sum_copy(hops[1] - 1, 1, a, True).wait_recv()
+        values.append(
+            total(hops[0] - 1, 0, a) + landed[hops[1] - 1, 2 * a + 1].astype(jnp.float32)
+        )
+    for a, value in enumerate(pointwise(*values)):
+        block(outs[a], me, 0)[...] = value
     for way, a in streams:
-        own_arrival(last, way, a).wait_recv()
-
-    def drain(step, carry):
-        for way, a in streams:
-            sum_copy(step, way, a, True).wait_send()
-            own_copy(step, way, a).wait_send()
-        return carry
-
-    lax.fori_loop(0, ring - 1, drain, 0)
+        own_copy(0, way, a).start()
+    run(own_forward, 1)
+    for way, a in streams:
+        own_arrival(hops[way] - 1, way, a).wait_recv()
+    run(drain, 0)
 
 
 def reduced_units(partials):
     ring = lax.axis_size("dp")
     rows, units = partials[0].shape
-    sems = pltpu.SemaphoreType.DMA((ring - 1, 6))
+    sems = pltpu.SemaphoreType.DMA((ring // 2, 6))
     return pl.pallas_call(
         functools.partial(ring_kernel, ring),
         out_shape=[jax.ShapeDtypeStruct((rows, units), jnp.bfloat16)] * 3,
         in_specs=[pl.BlockSpec(memory_space=pltpu.VMEM)] * 3,
         out_specs=[pl.BlockSpec(memory_space=pltpu.VMEM)] * 3,
         scratch_shapes=[
-            pltpu.VMEM((ring - 1, 6, rows // ring, units // 2), jnp.bfloat16),
+            pltpu.VMEM((ring // 2, 6, rows // ring, units), jnp.bfloat16),
             sems,
             sems,
             sems,

time: 217 us -> 221 us (1.018)
  Pallas kernels: 135 us -> 142 us
  starting transfers between devices: 8.58 us -> 5.89 us
    pallas_call x1, Pallas kernels: 135 us -> 142 us  [reduced_units(): pl.pallas_call(functools.partial(ring_kernel, ring), out_shape=[jax.Shape...]
    all_to_all x1, starting transfers between devices: 8.58 us -> 5.89 us  [swap(): lax.all_to_all(rows, 'expert', split_axis=0, concat_axis=0, tiled=True)]
where the time goes in v4:
time: 221 us
  Pallas kernels  142 us (64%)
  blocking collectives  29.9 us (14%)
  matrix products  21.3 us (10%)
  waiting for transfers between devices  13.3 us (6%)
  starting transfers between devices  5.89 us (3%)
  other arithmetic  3.93 us (2%)
  local copies, waits for them, and re-layouts  3.67 us (2%)
    pallas_call x1, Pallas kernels, reduced_units(): pl.pallas_call(functools.partial(ring_kernel, ring), out_shape=[jax.Shape...  142 us
    all_to_all x1, blocking collectives, swap(): lax.all_to_all(rows, 'expert', split_axis=0, concat_axis=0, tiled=True)  29.9 us
    dot_general x14, matrix products, dot_of(): lax.dot_general(first_op, second_op, (((first_dim,), (second_dim,)), ((),...  21.3 us
    all_to_all x1, waiting for transfers between devices, swap(): lax.all_to_all(rows, 'expert', split_axis=0, concat_axis=0, tiled=True)  13.3 us
    all_to_all x1, starting transfers between devices, swap(): lax.all_to_all(rows, 'expert', split_axis=0, concat_axis=0, tiled=True)  5.89 us
  transfers between devices with their start and end apart: 1, of which 1 were waited for; matrix products, arithmetic and copies ran while one was open for 3% of the time, Pallas kernels for 0%

profile of v4, /device:TPU:1, one launch (start us, length us, event | category | flops | bytes accessed | tf_op | source)
XLA Modules:
  0.0 220.7 jit_solution(6782654547767859228)
XLA Ops:
  0.6 0.0 copy-start
  0.6 0.8 fusion.20
  1.4 0.7 convert_bitcast_fusion
  2.1 0.7 select_reduce_fusion
  2.9 0.1 fusion.1
  3.0 0.1 iota.31
  3.1 0.2 fusion.6
  3.3 0.2 fusion.4
  3.6 1.2 convolution_convert_fusion.5
  4.8 1.2 convolution_convert_fusion.4
  6.0 0.1 pad_maximum_fusion
  6.1 0.7 copy.14
  6.8 0.0 copy-start.8
  6.8 29.9 %all_to_all.24 = bf16[32,40,512]{2,1,0:T(8,128)(2,1)S(1)} all-to-all(bf16[32,40,512]{2,1,0:T(8,128)(2,1)S(1)} %bitcast.60), channel_id=1, replica_groups=mesh['dp'=16,'expert'=32] {'expert'}, dimensions={0} | all-to-all | bytes 2621440 | tf_op jit(solution)/shard_map/all_to_all | solution.py:41
  36.7 2.0 convolution_convert_fusion.1.refs_1_
  38.7 2.0 convolution_convert_fusion.refs_2_
  40.7 0.0 copy-done.9
  40.7 1.9 convolution_convert_fusion.2.refs_0_
  42.7 141.9 %shard_map.110 = (bf16[1280,768]{1,0:T(8,128)(2,1)S(1)}, bf16[1280,768]{1,0:T(8,128)(2,1)S(1)}, bf16[1280,768]{1,0:T(8,128)(2,1)S(1)}) custom-call(bf16[1280,768]{1,0:T(8,128)(2,1)} %convolution_convert_fusion.2.refs_0_, bf16[1280,768]{1,0:T(8,128)(2,1)} %convolution_convert_fusion.1.refs_1_, bf16[1280,768]{1,0:T(8,128)(2,1)} %convolution_convert_fusion.refs_2_), custom_call_target="tpu_custom_call" | custom-call | tf_op jit(solution)/shard_map/pallas_call | solution.py:167
  184.6 0.7 convolution_convert_fusion.3
  185.4 0.7 fusion.17
  186.1 0.4 copy-done.2
  186.5 0.7 fusion
  187.2 1.2 pad_maximum_fusion.1
  188.4 2.4 %copy.15 = bf16[1280,512]{1,0:T(8,128)(2,1)} copy(bf16[1280,512]{0,1:T(8,128)(2,1)} %pad_maximum_fusion.1) | data formatting | bytes 2621440 | tf_op jit(solution)/shard_map/concatenate | solution.py:235
  190.8 5.9 %all-to-all-start.1 = ((bf16[32,40,512]{2,1,0:T(8,128)(2,1)}), bf16[32,40,512]{2,1,0:T(8,128)(2,1)}, u32[]{:S(2)}, u32[]{:S(2)}) async-start(bf16[32,40,512]{2,1,0:T(8,128)(2,1)} %bitcast.59), calls=%async_computation.1 | async-start | bytes 2621440 | tf_op jit(solution)/shard_map/all_to_all | solution.py:41
  196.8 3.4 %convolution_bitcast_fusion.2 = f32[1,256,768]{2,1,0:T(8,128)} fusion(bf16[1280,768]{1,0:T(8,128)(2,1)} %copy-done.1, bf16[1280,512]{1,0:T(8,128)(2,1)} %bitcast.56), kind=kOutput, calls=%fused_computation.12 | convolution fusion | flops 503316480 | bytes 3407872 | tf_op jit(solution)/shard_map/dot_general | solution.py:14
  200.2 1.6 convolution_bitcast_fusion.1
  201.8 1.6 convolution_bitcast_fusion
  203.4 13.3 %all-to-all-done.1 = bf16[32,40,512]{2,1,0:T(8,128)(2,1)} async-done(((bf16[32,40,512]{2,1,0:T(8,128)(2,1)}), bf16[32,40,512]{2,1,0:T(8,128)(2,1)}, u32[]{:S(2)}, u32[]{:S(2)}) %all-to-all-start.1) | async-done | bytes 1310752 | tf_op jit(solution)/shard_map/all_to_all | solution.py:41
  216.7 2.0 convolution_convert_fusion.6
  218.7 2.0 convolution_convert_fusion.7
  (17 shorter events, 0.0 us)
Async XLA Ops:
  0.6 38.1 %copy-start = (bf16[1,768,256]{2,1,0:T(8,128)(2,1)S(1)}, bf16[1,768,256]{2,1,0:T(8,128)(2,1)}, u32[]{:S(2)}) copy-start(bf16[1,768,256]{2,1,0:T(8,128)(2,1)} %param.12) | copy-start | bytes 1179652
  3.3 1.5 copy-start.6
  6.8 29.9 %copy-start.8 = (bf16[1,256,768]{2,1,0:T(8,128)(2,1)S(1)}, bf16[1,256,768]{2,1,0:T(8,128)(2,1)}, u32[]{:S(2)}) copy-start(bf16[1,256,768]{2,1,0:T(8,128)(2,1)} %param.11) | copy-start | bytes 1179652
  36.7 4.0 %copy-start.4 = (bf16[32,40,512]{2,1,0:T(8,128)(2,1)}, bf16[32,40,512]{2,1,0:T(8,128)(2,1)S(1)}, u32[]{:S(2)}) copy-start(bf16[32,40,512]{2,1,0:T(8,128)(2,1)S(1)} %all_to_all.24) | copy-start | bytes 3932164
  38.7 2.0 copy-start.9
  184.6 1.5 copy-start.1
  184.6 1.9 copy-start.2
  190.8 25.8 %all-to-all-start.1 = ((bf16[32,40,512]{2,1,0:T(8,128)(2,1)}), bf16[32,40,512]{2,1,0:T(8,128)(2,1)}, u32[]{:S(2)}, u32[]{:S(2)}) async-start(bf16[32,40,512]{2,1,0:T(8,128)(2,1)} %bitcast.59), calls=%async_computation.1 | async-start | bytes 2621440 | tf_op jit(solution)/shard_map/all_to_all | solution.py:41
  196.7 3.4 %copy-start.5 = (bf16[32,40,512]{2,1,0:T(8,128)(2,1)S(1)}, bf16[32,40,512]{2,1,0:T(8,128)(2,1)}, u32[]{:S(2)}) copy-start(bf16[32,40,512]{2,1,0:T(8,128)(2,1)} %copy-done.4) | copy-start | bytes 3932164
  200.2 1.6 copy-start.3
  201.8 14.9 %copy-start.7 = (bf16[1280,128]{1,0:T(8,128)(2,1)S(1)}, bf16[1280,128]{1,0:T(8,128)(2,1)}, u32[]{:S(2)}) copy-start(bf16[1280,128]{1,0:T(8,128)(2,1)} %copy-done.6) | copy-start | bytes 983044
